TPU v7x, 512 devices: a whole 4x8x8 slice. The times are simulated.
512 devices in a mesh: cfg: 2 (over z_lo), rs: 32 (over x, z_hi, core), tp: 8 (over y).
Axes of the slice: x: 4, y: 8, z: 8 (z_hi: 4, z_lo: 2; z = z_hi * 2 + z_lo), core: 2. Of those that a mesh axis runs over, the one named last changes fastest.
Arguments:
- latents: float32 [8192, 2, 16], P('rs'), may hold values from -6 to 6
- timesteps: int32 [8, 2], replicated, may hold values from 0 to 249
- labels: int32 [8, 2], replicated, may hold values from 0 to 999
- solver_table: float32 [250, 2], replicated, may hold values from 0.5 to 1.5
- time_table: bfloat16 [250, 1152], P(None, 'tp'), may hold values from -6 to 6
- label_table: bfloat16 [1001, 1152], P(None, 'tp'), may hold values from -6 to 6
- patch_weight: bfloat16 [16, 1152], replicated, may hold values from -1.5 to 1.5
- patch_bias: float32 [1152], replicated, may hold values from -3 to 3
- modulation_weight: bfloat16 [9216, 1152], P(('rs', 'tp')), may hold values from -0.1875 to 0.1875
- modulation_bias: float32 [9216], P(('rs', 'tp')), may hold values from -3 to 3
- heads_weight: bfloat16 [1, 1152, 3, 1152], P(None, None, None, 'tp'), may hold values from -0.375 to 0.375
- heads_bias: float32 [1, 3, 1152], P(None, None, 'tp'), may hold values from -1.75 to 1.75
- output_weight: bfloat16 [1, 1152, 1152], P(None, 'tp'), may hold values from -0.1875 to 0.1875
- output_bias: float32 [1, 1152], replicated, may hold values from -1.75 to 1.75
- up_weight: bfloat16 [1, 1152, 4608], P(None, None, 'tp'), may hold values from -0.1875 to 0.1875
- up_bias: float32 [1, 4608], P(None, 'tp'), may hold values from -1.75 to 1.75
- down_weight: bfloat16 [1, 4608, 1152], P(None, 'tp'), may hold values from -0.09375 to 0.09375
- down_bias: float32 [1, 1152], replicated, may hold values from -1.75 to 1.75
- final_weight: bfloat16 [1152, 16], replicated, may hold values from -0.1875 to 0.1875
- final_bias: float32 [16], replicated, may hold values from -1.75 to 1.75
Outputs:
- next_latents: float32 [8192, 2, 16], P(('rs', 'tp'), None, 'cfg')
All inputs are finite; a program needn't handle non-finite values.
Results may differ from a plain program's by a relative error of at most 0.02.
Values may be sent and summed in bfloat16 or wider, within the bound.
A program may use at most 64 MiB of HBM per device.

v0:
```python
import jax
import jax.numpy as jnp
from jax import lax
from jax.sharding import PartitionSpec as P

HEAD_DIM = 72
GRID = 32
LAYERS = 1
guidance = 4.0


def partner_2(value, axis, stride):
    mask = 2**stride
    pairs = [(source, source ^ mask) for source in range(lax.axis_size(axis))]
    return lax.ppermute(value, axis, pairs)


def layer_norm(values):
    centre = values - jnp.mean(values, axis=-1, keepdims=True)
    spread = jnp.mean(centre * centre, axis=-1, keepdims=True)
    return centre * lax.rsqrt(spread + 1e-06)


def position_rows(token_index, grid_side, model_width):
    freq_count = model_width // 4
    frequency = 1.0 / 10000.0 ** (jnp.arange(freq_count, dtype=jnp.float32) / freq_count)
    row_angle = (token_index // grid_side).astype(jnp.float32)[:, None] * frequency[None, :]
    col_angle = (token_index % grid_side).astype(jnp.float32)[:, None] * frequency[None, :]
    return jnp.concatenate(
        [jnp.sin(row_angle), jnp.cos(row_angle), jnp.sin(col_angle), jnp.cos(col_angle)], axis=1
    )


def modulate(stream, modulation, offset):
    return (
        layer_norm(stream) * (1.0 + modulation[None, :, offset + 1]) + modulation[None, :, offset]
    ).astype(jnp.bfloat16)


def project_heads(normed, weight, bias):
    row_count, latents_dev, model_width = normed.shape
    flattened = normed.reshape(row_count * latents_dev, model_width)
    result = jnp.dot(
        flattened, weight.reshape(model_width, -1), preferred_element_type=jnp.float32
    ) + bias.reshape(-1)
    return result.astype(jnp.bfloat16).reshape(row_count, latents_dev, -1)


def hidden_units(normed, weight, bias):
    row_count, latents_dev, model_width = normed.shape
    flattened = normed.reshape(row_count * latents_dev, model_width)
    preact = jnp.dot(flattened, weight, preferred_element_type=jnp.float32) + bias
    return (
        jax.nn.gelu(preact, approximate=True)
        .astype(jnp.bfloat16)
        .reshape(row_count, latents_dev, -1)
    )


def attend_block(queries, key_block, columns):
    key_count, latents_dev = (key_block.shape[0], key_block.shape[1])
    head_count, head_size = (queries.shape[2], queries.shape[3])
    key_rows = key_block[..., :columns].reshape(key_count, latents_dev, head_count, head_size)
    value_rows = key_block[..., columns:].reshape(key_count, latents_dev, head_count, head_size)
    scores = jnp.einsum(
        "qlhd,klhd->lhqk", queries, key_rows, preferred_element_type=jnp.float32
    ) * head_size ** (-0.5)
    row_top = jnp.max(scores, axis=-1)
    exponent = jnp.exp(scores - row_top[..., None])
    row_total = jnp.sum(exponent, axis=-1)
    weighted = jnp.einsum(
        "lhqk,klhd->lhqd",
        exponent.astype(jnp.bfloat16),
        value_rows,
        preferred_element_type=jnp.float32,
    )
    return (row_top, row_total, weighted)


def merge_blocks(first, second):
    row_top = jnp.maximum(first[0], second[0])
    left_scale = jnp.exp(first[0] - row_top)
    right_scale = jnp.exp(second[0] - row_top)
    row_total = first[1] * left_scale + second[1] * right_scale
    weighted = first[2] * left_scale[..., None] + second[2] * right_scale[..., None]
    return (row_top, row_total, weighted)


def attention(projected, columns, head_size):
    row_count, latents_dev = (projected.shape[0], projected.shape[1])
    queries = projected[..., :columns].reshape(
        row_count, latents_dev, columns // head_size, head_size
    )
    own_block = projected[..., columns:]
    running = attend_block(queries, own_block, columns)
    near_block = partner_2(own_block, "rs", 0)
    running = merge_blocks(running, attend_block(queries, near_block, columns))
    far_block = partner_2(jnp.concatenate([own_block, near_block], axis=0), "rs", 1)
    running = merge_blocks(running, attend_block(queries, far_block, columns))
    result = running[2] / running[1][..., None]
    return (
        jnp.transpose(result, (2, 0, 1, 3))
        .reshape(row_count, latents_dev, columns)
        .astype(jnp.bfloat16)
    )


def per_device(
    latents,
    timesteps,
    labels,
    solver_table,
    time_table,
    label_table,
    patch_weight,
    patch_bias,
    modulation_weight,
    modulation_bias,
    heads_weight,
    heads_bias,
    output_weight,
    output_bias,
    up_weight,
    up_bias,
    down_weight,
    down_bias,
    final_weight,
    final_bias,
):
    tp_count = lax.axis_size("tp")
    tp_index = lax.axis_index("tp")
    half_index = lax.axis_index("cfg")
    rs_index = lax.axis_index("rs")
    group_index = rs_index // 4
    quarter = rs_index % 4
    local_tokens, latents_dev, patch_width = latents.shape
    model_width = patch_weight.shape[1]
    share_rows = local_tokens // tp_count
    classes = label_table.shape[0] - 1
    columns = heads_weight.shape[3]
    steps_all = timesteps.reshape(-1)
    class_ids = jnp.where(half_index == 0, labels.reshape(-1), classes)
    step_onehot = jax.nn.one_hot(steps_all, time_table.shape[0], dtype=jnp.bfloat16)
    class_onehot = jax.nn.one_hot(class_ids, classes + 1, dtype=jnp.bfloat16)
    condition_part = jnp.dot(step_onehot, time_table, preferred_element_type=jnp.float32) + jnp.dot(
        class_onehot, label_table, preferred_element_type=jnp.float32
    )
    condition = lax.all_gather(condition_part, "tp", axis=1, tiled=True)
    activation = jax.nn.silu(condition).astype(jnp.bfloat16)
    modulation_part = (
        lax.dot_general(
            activation,
            modulation_weight,
            (((1,), (1,)), ((), ())),
            preferred_element_type=jnp.float32,
        )
        + modulation_bias
    )
    modulation_all = lax.all_gather(modulation_part, ("rs", "tp"), axis=1, tiled=True)
    modulation_all = modulation_all.reshape(timesteps.shape[0], latents_dev, -1, model_width)
    modulation = lax.dynamic_index_in_dim(modulation_all, group_index, 0, keepdims=False)
    token_index = quarter * local_tokens + jnp.arange(local_tokens, dtype=jnp.int32)
    position = position_rows(token_index, GRID, model_width)
    own_latents = lax.dynamic_slice_in_dim(latents, tp_index * share_rows, share_rows, 0)
    flattened = latents.reshape(-1, patch_width).astype(jnp.bfloat16)
    embedded = jnp.dot(flattened, patch_weight, preferred_element_type=jnp.float32) + patch_bias
    stream = embedded.reshape(latents.shape[0], latents_dev, model_width) + position[:, None, :]
    projected = project_heads(modulate(stream, modulation, 0), heads_weight[0], heads_bias[0])
    attended = attention(projected, columns, HEAD_DIM).reshape(-1, columns)
    head_terms = jnp.dot(attended, output_weight[0], preferred_element_type=jnp.float32)
    attn_out = (
        lax.psum(head_terms.astype(jnp.bfloat16), "tp")
        .astype(jnp.float32)
        .reshape(local_tokens, latents_dev, model_width)
    )
    stream = stream + modulation[None, :, 2] * (attn_out + output_bias[0])
    hidden = hidden_units(modulate(stream, modulation, 3), up_weight[0], up_bias[0])
    unit_terms = jnp.dot(
        hidden.reshape(-1, hidden.shape[2]), down_weight[0], preferred_element_type=jnp.float32
    )
    mlp_out = (
        lax.psum(unit_terms.astype(jnp.bfloat16), "tp")
        .astype(jnp.float32)
        .reshape(local_tokens, latents_dev, model_width)
    )
    stream = stream + modulation[None, :, 5] * (mlp_out + down_bias[0])
    own_stream = lax.dynamic_slice_in_dim(stream, tp_index * share_rows, share_rows, 0)
    final_normed = modulate(own_stream, modulation, 6 * LAYERS)
    noise_pred = (
        jnp.dot(
            final_normed.reshape(-1, model_width), final_weight, preferred_element_type=jnp.float32
        )
        + final_bias
    )
    noise_pred = noise_pred.reshape(share_rows, latents_dev, patch_width)
    half_width = patch_width // 2
    kept_half = lax.dynamic_slice_in_dim(noise_pred, half_index * half_width, half_width, 2)
    sent_half = lax.dynamic_slice_in_dim(noise_pred, (1 - half_index) * half_width, half_width, 2)
    partner = partner_2(sent_half, "cfg", 0)
    conditional = jnp.where(half_index == 0, kept_half, partner)
    unconditional = jnp.where(half_index == 0, partner, kept_half)
    guided = unconditional + guidance * (conditional - unconditional)
    own_channels = lax.dynamic_slice_in_dim(own_latents, half_index * half_width, half_width, 2)
    step_own = lax.dynamic_index_in_dim(timesteps, group_index, 0, keepdims=False)
    step_hot_own = jax.nn.one_hot(step_own, solver_table.shape[0], dtype=jnp.float32)
    coefficients = jnp.dot(step_hot_own, solver_table, precision=lax.Precision.HIGHEST)
    return coefficients[None, :, 0:1] * own_channels + coefficients[None, :, 1:2] * guided


def solution(mesh):
    in_specs = (
        P("rs", None, None),
        P(),
        P(),
        P(),
        P(None, "tp"),
        P(None, "tp"),
        P(),
        P(),
        P(("rs", "tp"), None),
        P(("rs", "tp")),
        P(None, None, None, "tp"),
        P(None, None, "tp"),
        P(None, "tp", None),
        P(),
        P(None, None, "tp"),
        P(None, "tp"),
        P(None, "tp", None),
        P(),
        P(),
        P(),
    )
    out_specs = P(("rs", "tp"), None, "cfg")
    return jax.shard_map(
        per_device, mesh=mesh, in_specs=in_specs, out_specs=out_specs, check_vma=False
    )
```

profile of v0, /device:TPU:2, one launch (start us, length us, event | category | flops | bytes accessed | tf_op | source)
XLA Modules:
  0.0 997.7 jit_solution(18414856131837989022)
XLA Ops:
  6.6 3.8 multiply_cosine_fusion
  10.4 1.6 concatenate.6
  12.0 2.2 add.308
  14.2 4.0 add.314
  18.4 3.6 fusion.90
  22.1 1.4 copy-done.1
  24.6 26.2 %all-gather = f32[8,144,16]{1,2,0:T(8,128)S(1)} all-gather(f32[1,144,16]{1,2,0:T(8,128)S(1)} %fusion.29), channel_id=1, replica_groups=mesh['cfg'=2,'rs'=32,'tp'=8] {'tp'}, dimensions={0}, use_global_device_ids=true | all-gather | bytes 82944 | tf_op jit(solution)/shard_map/all_gather | solution.py:148
  51.2 616.4 %all-gather.1 = f32[256,36,16]{1,2,0:T(8,128)S(1)} all-gather(f32[1,36,16]{1,2,0:T(8,128)S(1)} %fusion.30), channel_id=1, replica_groups=mesh['cfg'=2,'rs'=32,'tp'=8] {'rs','tp'}, dimensions={0}, use_global_device_ids=true | all-gather | bytes 592128 | tf_op jit(solution)/shard_map/all_gather | solution.py:159
  667.6 0.7 copy.75
  668.3 2.4 reshape.290
  670.7 1.2 copy.101
  672.6 2.1 add.320
  674.7 4.0 add.321
  678.7 2.1 mul.284
  680.8 4.1 mul.285
  685.0 4.1 fusion.4
  690.2 1.9 collective-permute-start
  692.1 0.8 fusion.92
  692.9 0.8 copy.78
  694.1 1.3 fusion.95
  695.4 0.8 fusion.34
  696.1 2.2 pad_maximum_fusion
  698.3 2.0 copy.84
  700.4 2.1 collective-permute-start.1
  702.5 1.5 fusion.93
  704.2 0.8 copy.82
  705.6 26.2 %collective-permute-done.1 = bf16[512,2,288]{0,2,1:T(8,128)(2,1)} collective-permute-done((bf16[512,2,288]{0,2,1:T(8,128)(2,1)}, bf16[512,2,288]{0,2,1:T(8,128)(2,1)}, u32[]{:S(2)}, u32[]{:S(2)}) %collective-permute-start.1) | collective-permute-done | bytes 589856 | tf_op jit(solution)/shard_map/ppermute | solution.py:15
  731.8 1.1 fusion.91
  735.8 1.5 convolution_convert_fusion
  737.4 2.1 mul.280
  739.4 4.1 mul.306
  743.5 2.1 add.341
  745.6 4.0 add.342
  749.7 2.0 mul.311
  751.7 4.1 mul.312
  755.7 133.0 %all-reduce.3.cloned.1.call-done = bf16[512,1152]{1,0:T(8,128)(2,1)} async-done(((bf16[512,1152]{1,0:T(8,128)(2,1)}), bf16[512,1152]{1,0:T(8,128)(2,1)}) %all-reduce.3.cloned.1.call-update) | async-done | bytes 1179664 | tf_op jit(solution)/shard_map/psum | solution.py:172
  888.8 3.2 fusion.85
  891.9 1.4 copy-done.2
  893.7 5.7 convolution_convert_fusion.1
  899.5 1.3 reshape.283
  901.0 4.1 reshape.272
  905.3 0.9 constant_dynamic-slice_fusion.2
  906.3 2.2 reshape.282
  908.5 73.4 %all-reduce.5.cloned.1.call-done = bf16[256,2,1152]{2,1,0:T(2,128)(2,1)} async-done(((bf16[256,2,1152]{2,1,0:T(2,128)(2,1)}), bf16[256,2,1152]{2,1,0:T(2,128)(2,1)}) %all-reduce.5.cloned.1.call-update) | async-done | bytes 1179664 | tf_op jit(solution)/shard_map/psum | solution.py:182
  981.9 1.6 fusion.83
  984.7 3.6 collective-permute-start.2
  988.5 1.7 collective-permute-done.2
  990.2 0.7 multiply_add_fusion.1
  (120 shorter events, 9.7 us)
Async XLA Ops:
  6.5 887.2 %copy-start = (bf16[1,576,1152]{2,1,0:T(8,128)(2,1)S(1)}, bf16[1,576,1152]{2,1,0:T(8,128)(2,1)}, u32[]{:S(2)}) copy-start(bf16[1,576,1152]{2,1,0:T(8,128)(2,1)} %param.36) | copy-start | bytes 3981316
  6.5 882.2 %all-reduce.3.cloned.1.call-start = ((), (), s32[]{:S(2)}) async-start(), calls=%async_computation | async-start | bytes 2359296 | tf_op jit(solution)/shard_map/psum | solution.py:172
  12.0 6.3 copy-start.3
  14.2 4.1 copy-start.10
  14.2 4.2 copy-start.11
  14.2 4.2 copy-start.14
  22.1 1.4 copy-start.1
  22.1 1.8 copy-start.21
  22.1 2.0 copy-start.17
  22.1 2.2 copy-start.23
  22.1 2.3 copy-start.8
  22.1 28.9 %copy-start.22 = (bf16[36,1152]{1,0:T(8,128)(2,1)S(1)}, bf16[36,1152]{1,0:T(8,128)(2,1)}, u32[]{:S(2)}) copy-start(bf16[36,1152]{1,0:T(8,128)(2,1)} %param.28) | copy-start | bytes 248836
  22.1 28.9 %copy-start.26 = (f32[36]{0:T(128)S(1)}, f32[36]{0:T(128)}, u32[]{:S(2)}) copy-start(f32[36]{0:T(128)} %param.29) | copy-start | bytes 436
  680.8 4.1 copy-start.19
  680.8 4.2 copy-start.6
  690.2 5.9 copy-start.5
  690.2 5.9 collective-permute-start
  700.4 31.5 %collective-permute-start.1 = (bf16[512,2,288]{0,2,1:T(8,128)(2,1)}, bf16[512,2,288]{0,2,1:T(8,128)(2,1)}, u32[]{:S(2)}, u32[]{:S(2)}) collective-permute-start(bf16[512,2,288]{0,2,1:T(8,128)(2,1)} %copy.84), channel_id=1, source_target_pairs={{0,16},{8,24},{16,0},{24,8},{32,48},{40,56},{48,32},{56,40},{64,80... | collective-permute-start | bytes 1769480 | tf_op jit(solution)/shard_map/ppermute | solution.py:15
  732.9 1.2 copy-start.13
  734.1 1.0 copy-start.9
  734.5 1.3 copy-start.7
  737.3 244.6 %all-reduce.5.cloned.1.call-start = ((), (), s32[]{:S(2)}) async-start(), calls=%async_computation.1 | async-start | bytes 2359296 | tf_op jit(solution)/shard_map/psum | solution.py:182
  739.4 4.1 copy-start.15
  739.4 4.1 copy-start.12
  751.7 4.1 copy-start.20
  891.9 1.4 copy-start.2
  899.5 1.4 copy-start.18
  901.0 4.1 copy-start.16
  901.0 4.1 copy-start.25
  901.0 5.2 copy-start.4
  906.3 77.9 %copy-start.24 = (bf16[1152,16]{0,1:T(8,128)(2,1)S(1)}, bf16[1152,16]{0,1:T(8,128)(2,1)}, u32[]{:S(2)}) copy-start(bf16[1152,16]{0,1:T(8,128)(2,1)} %param.38) | copy-start | bytes 110596
  906.3 77.9 %copy-start.27 = (f32[16]{0:T(128)S(1)}, f32[16]{0:T(128)}, u32[]{:S(2)}) copy-start(f32[16]{0:T(128)} %param.39) | copy-start | bytes 196
  984.7 5.5 collective-permute-start.2
Sparse Core Ops, SparseCore 0:
  737.4 151.2 all-reduce.2
  900.9 80.9 all-reduce.4
where the time goes:
time: 999 us; the launch traced here: 998 us
  blocking collectives  643 us (64%)
  waiting for transfers between devices  234 us (23%)
  local copies, waits for them, and re-layouts  64.7 us (6%)
  matrix products  19.2 us (2%)
  other arithmetic  15.1 us (2%)
  between operations  14 us (1%)
    all_gather x1, blocking collectives, per_device(): lax.all_gather(modulation_part, ('rs', 'tp'), axis=1, tiled=True)  616 us
    psum x1, waiting for transfers between devices, per_device(): lax.psum(head_terms.astype(jnp.bfloat16), 'tp').astype(jnp.float32)  133 us
    psum x1, waiting for transfers between devices, per_device(): lax.psum(unit_terms.astype(jnp.bfloat16), 'tp').astype(jnp.float32)  73.4 us
    ppermute x3, waiting for transfers between devices, partner_2(): return lax.ppermute(value, axis, pairs)  28 us
    all_gather x1, blocking collectives, per_device(): condition = lax.all_gather(condition_part, 'tp', axis=1, tiled=True)  26.2 us
  transfers between devices with their start and end apart: 5, of which 4 were waited for; matrix products, arithmetic and copies ran while one was open for 3% of the time, Pallas kernels for 0%

commit v1 on v0

--- a/solution.py
+++ b/solution.py
@@ -156,7 +156,12 @@
         )
         + modulation_bias
     )
-    modulation_all = lax.all_gather(modulation_part, ("rs", "tp"), axis=1, tiled=True)
+    modulation_all = jnp.concatenate(
+        lax.all_to_all(
+            jnp.stack([modulation_part] * lax.axis_size(("rs", "tp"))), ("rs", "tp"), 0, 0
+        ),
+        axis=1,
+    )
     modulation_all = modulation_all.reshape(timesteps.shape[0], latents_dev, -1, model_width)
     modulation = lax.dynamic_index_in_dim(modulation_all, group_index, 0, keepdims=False)
     token_index = quarter * local_tokens + jnp.arange(local_tokens, dtype=jnp.int32)

time: 999 us -> 355 us (0.36)
  blocking collectives: 643 us -> 26.2 us
  waiting for transfers between devices: 234 us -> 164 us
  starting transfers between devices: 7.65 us -> 30.3 us
    all_gather x1 -> x0, blocking collectives: 616 us -> none  [per_device(): lax.all_gather(modulation_part, ('rs', 'tp'), axis=1, tiled=True)]
    psum x1, waiting for transfers between devices: 133 us -> 58.4 us  [per_device(): lax.psum(head_terms.astype(jnp.bfloat16), 'tp').astype(jnp.float32)]
    all_to_all x0 -> x1, starting transfers between devices: none -> 20.2 us  [per_device(): lax.all_to_all(jnp.stack([modulation_part] * lax.axis_size(('rs', 'tp')))...]
  transfers between devices with their start and end apart: 5 -> 6, of which waited for: 4 -> 5; matrix products, arithmetic and copies ran while one was open for 3% -> 14% of each run, Pallas kernels for 0% -> 0%
where the time goes in v1:
time: 355 us; the launch traced here: 348 us
  waiting for transfers between devices  164 us (46%)
  local copies, waits for them, and re-layouts  72.5 us (20%)
  starting transfers between devices  30.3 us (9%)
  blocking collectives  26.2 us (7%)
  matrix products  22 us (6%)
  other arithmetic  19.2 us (5%)
  between operations  14.2 us (4%)
    psum x1, waiting for transfers between devices, per_device(): lax.psum(unit_terms.astype(jnp.bfloat16), 'tp').astype(jnp.float32)  73.4 us
    psum x1, waiting for transfers between devices, per_device(): lax.psum(head_terms.astype(jnp.bfloat16), 'tp').astype(jnp.float32)  58.4 us
    all_gather x1, blocking collectives, per_device(): condition = lax.all_gather(condition_part, 'tp', axis=1, tiled=True)  26.2 us
    ppermute x3, waiting for transfers between devices, partner_2(): return lax.ppermute(value, axis, pairs)  26 us
    all_to_all x1, starting transfers between devices, per_device(): lax.all_to_all(jnp.stack([modulation_part] * lax.axis_size(('rs', 'tp')))...  20.2 us
    mul x4, local copies, waits for them, and re-layouts, modulate(): layer_norm(stream) * (1.0 + modulation[None, :, offset + 1])  12.4 us
    add x4, local copies, waits for them, and re-layouts, modulate(): layer_norm(stream) * (1.0 + modulation[None, :, offset + 1])  12.2 us
    ppermute x3, starting transfers between devices, partner_2(): return lax.ppermute(value, axis, pairs)  9.53 us
  transfers between devices with their start and end apart: 6, of which 5 were waited for; matrix products, arithmetic and copies ran while one was open for 14% of the time, Pallas kernels for 0%

profile of v1, /device:TPU:2, one launch (start us, length us, event | category | flops | bytes accessed | tf_op | source)
XLA Modules:
  0.0 348.4 jit_solution(13364339527754651292)
XLA Ops:
  8.3 1.0 fusion.59
  9.4 1.2 fusion.29
  10.6 26.2 %all-gather = f32[8,144,16]{1,2,0:T(8,128)S(1)} all-gather(f32[1,144,16]{1,2,0:T(8,128)S(1)} %fusion.29), channel_id=1, replica_groups=mesh['cfg'=2,'rs'=32,'tp'=8] {'tp'}, dimensions={0}, use_global_device_ids=true | all-gather | bytes 82944 | tf_op jit(solution)/shard_map/all_gather | solution.py:148
  36.9 1.0 convolution_add_fusion.5
  38.1 2.9 reshape.299
  41.0 20.2 %all-to-all-start = ((f32[256,1,576]{2,1,0:T(1,128)}), f32[256,1,576]{2,1,0:T(1,128)S(1)}, u32[]{:S(2)}, u32[]{:S(2)}) async-start(f32[256,1,576]{2,1,0:T(1,128)} %reshape.299), calls=%async_computation | async-start | bytes 1310720 | tf_op jit(solution)/shard_map/all_to_all | solution.py:160
  61.8 3.8 %multiply_cosine_fusion = (f32[256,288]{1,0:T(8,128)S(1)}, f32[256,288]{1,0:T(8,128)}, f32[256,288]{1,0:T(8,128)}, f32[256,288]{1,0:T(8,128)}) fusion(f32[256]{0:T(256)S(1)} %get-tuple-element.48, f32[288]{0:T(512)S(1)} %negate_power_fusion, f32[256]{0:T(256)S(1)} %get-tuple-element.49), kind=kLoop, calls=%fused_computation.61 | loop fusion | flops 147456 | bytes 1182848 | tf_op jit(solution)/shard_map/cos | solution.py:30
  65.6 1.7 concatenate.6
  67.3 2.2 add.308
  69.6 4.1 %add.314 = f32[512,1152]{1,0:T(8,128)} reshape(f32[256,2,1152]{2,1,0:T(2,128)} %add.308) | data formatting | bytes 4718592 | tf_op jit(solution)/shard_map/add | solution.py:172
  73.9 3.6 %fusion.89 = (f32[512]{0:T(512)S(1)}, f32[512,1152]{1,0:T(8,128)S(1)}, f32[512,1152]{1,0:T(8,128)}) fusion(f32[512,1152]{1,0:T(8,128)} %add.314, f32[1152]{0:T(1024)S(1)} %copy-done.13, bf16[512,16]{1,0:T(8,128)(2,1)S(1)} %bitcast.172, bf16[16,1152]{1,0:T(8,128)(2,1)S(1)} %copy-done.10), kind=kOutput, calls=%fused_computation.152 | convolution fusion | flops 20643328 | bytes 7137792 | tf_op jit(solution)/shard_map/dot_general | solution.py:171
  77.6 1.4 copy-done.1
  79.3 6.2 %all-to-all-done = f32[256,1,576]{2,1,0:T(1,128)S(1)} async-done(((f32[256,1,576]{2,1,0:T(1,128)}), f32[256,1,576]{2,1,0:T(1,128)S(1)}, u32[]{:S(2)}, u32[]{:S(2)}) %all-to-all-start) | async-done | bytes 589856 | tf_op jit(solution)/shard_map/all_to_all | solution.py:160
  86.0 3.3 reduce.14
  89.3 2.5 reshape.300
  91.8 2.0 copy.74
  93.8 2.9 reshape_reshape.3
  97.4 2.1 add.320
  99.4 4.0 %add.321 = f32[512,1152]{1,0:T(8,128)} reshape(f32[256,2,1152]{2,1,0:T(2,128)} %add.320) | data formatting | bytes 4718592 | tf_op jit(solution)/shard_map/add | solution.py:36
  103.5 2.1 mul.284
  105.5 4.3 %mul.285 = f32[512,1152]{1,0:T(8,128)} reshape(f32[256,2,1152]{2,1,0:T(2,128)} %mul.284) | data formatting | bytes 4718592 | tf_op jit(solution)/shard_map/mul | solution.py:36
  109.8 4.1 %fusion.4 = bf16[512,432]{0,1:T(8,128)(2,1)S(1)} fusion(bf16[1152,432]{0,1:T(8,128)(2,1)S(1)} %bitcast.168, f32[512,1152]{1,0:T(8,128)} %add.321, f32[512,1152]{1,0:T(8,128)} %mul.285, f32[512,1152]{1,0:T(8,128)} %copy-done.1, f32[512]{0:T(512)S(1)} %add_rsqrt_fusion.2, f32[512]{0:T(512)S(1)} %broadcast_multiply_fusion.2, f32[432]{0:T(512)S(1)} %add.323), kind=kOutput, calls=%fused_computation.19 | convolution fusion | flops 512999424 | bytes 8521408 | tf_op jit(solution)/shard_map/dot_general | solution.py:43
  116.8 1.9 collective-permute-start
  118.9 1.3 fusion.94
  120.9 2.2 pad_maximum_fusion
  123.1 2.0 copy.83
  125.2 4.1 %collective-permute-start.1 = (bf16[512,2,288]{0,2,1:T(8,128)(2,1)}, bf16[512,2,288]{0,2,1:T(8,128)(2,1)}, u32[]{:S(2)}, u32[]{:S(2)}) collective-permute-start(bf16[512,2,288]{0,2,1:T(8,128)(2,1)} %copy.83), channel_id=1, source_target_pairs={{0,16},{8,24},{16,0},{24,8},{32,48},{40,56},{48,32},{56,40},{64,80... | collective-permute-start | bytes 1769480 | tf_op jit(solution)/shard_map/ppermute | solution.py:15
  129.3 1.5 fusion.92
  132.3 24.3 %collective-permute-done.1 = bf16[512,2,288]{0,2,1:T(8,128)(2,1)} collective-permute-done((bf16[512,2,288]{0,2,1:T(8,128)(2,1)}, bf16[512,2,288]{0,2,1:T(8,128)(2,1)}, u32[]{:S(2)}, u32[]{:S(2)}) %collective-permute-start.1) | collective-permute-done | bytes 589856 | tf_op jit(solution)/shard_map/ppermute | solution.py:15
  156.7 1.1 fusion.90
  160.6 1.5 convolution_convert_fusion
  162.3 2.1 mul.280
  164.3 4.2 %mul.306 = f32[512,1152]{1,0:T(8,128)} reshape(f32[256,2,1152]{2,1,0:T(2,128)} %mul.280) | data formatting | bytes 4718592 | tf_op jit(solution)/shard_map/mul | solution.py:181
  168.6 2.1 add.341
  170.6 4.1 %add.342 = f32[512,1152]{1,0:T(8,128)} reshape(f32[256,2,1152]{2,1,0:T(2,128)} %add.341) | data formatting | bytes 4718592 | tf_op jit(solution)/shard_map/add | solution.py:36
  174.7 2.0 mul.311
  176.7 4.1 %mul.312 = f32[512,1152]{1,0:T(8,128)} reshape(f32[256,2,1152]{2,1,0:T(2,128)} %mul.311) | data formatting | bytes 4718592 | tf_op jit(solution)/shard_map/mul | solution.py:36
  180.8 58.4 %all-reduce.3.cloned.1.call-done = bf16[512,1152]{1,0:T(8,128)(2,1)} async-done(((bf16[512,1152]{1,0:T(8,128)(2,1)}), bf16[512,1152]{1,0:T(8,128)(2,1)}) %all-reduce.3.cloned.1.call-update) | async-done | bytes 1179664 | tf_op jit(solution)/shard_map/psum | solution.py:177
  239.2 3.2 fusion.84
  242.4 1.4 copy-done.2
  244.2 5.7 %convolution_convert_fusion.1 = bf16[512,1152]{1,0:T(8,128)(2,1)S(1)} fusion(bf16[1,576,1152]{2,1,0:T(8,128)(2,1)S(1)} %copy-done, bf16[1,1152,576]{1,2,0:T(8,128)(2,1)} %param.34, f32[512,1152]{1,0:T(8,128)} %add.342, f32[512,1152]{1,0:T(8,128)} %mul.312, f32[512,1152]{1,0:T(8,128)} %copy-done.2, f32[512]{0:T(512)S(1)} %add_rsqrt_fusion.1, ...), kind=kOutput, calls=%fused_computation.2 | convolution fusion | flops 1365442560 | bytes 10918144 | tf_op jit(solution)/shard_map/dot_general | solution.py:183
  249.9 1.3 reshape.285
  251.5 4.1 %reshape.274 = f32[256,2,1152]{2,1,0:T(2,128)} reshape(f32[512,1152]{1,0:T(8,128)} %get-tuple-element.41) | data formatting | bytes 4718592 | tf_op jit(solution)/shard_map/reshape | solution.py:172
  256.7 2.2 reshape.284
  258.9 73.4 %all-reduce.5.cloned.1.call-done = bf16[256,2,1152]{2,1,0:T(2,128)(2,1)} async-done(((bf16[256,2,1152]{2,1,0:T(2,128)(2,1)}), bf16[256,2,1152]{2,1,0:T(2,128)(2,1)}) %all-reduce.5.cloned.1.call-update) | async-done | bytes 1179664 | tf_op jit(solution)/shard_map/psum | solution.py:187
  332.3 1.6 fusion.82
  335.1 3.6 %collective-permute-start.2 = (f32[32,2,8]{0,2,1:T(8,128)S(1)}, f32[32,2,8]{0,2,1:T(8,128)S(1)}, u32[]{:S(2)}, u32[]{:S(2)}) collective-permute-start(f32[32,2,8]{0,2,1:T(8,128)S(1)} %copy.98), channel_id=1, source_target_pairs={{0,256},{256,0},{1,257},{257,1},{2,258},{258,2},{3,259},{259,3},{4... | collective-permute-start | bytes 6152 | tf_op jit(solution)/shard_map/ppermute | solution.py:15
  338.9 1.7 collective-permute-done.2
  (113 shorter events, 16.5 us)
Async XLA Ops:
  6.5 237.6 %copy-start = (bf16[1,576,1152]{2,1,0:T(8,128)(2,1)S(1)}, bf16[1,576,1152]{2,1,0:T(8,128)(2,1)}, u32[]{:S(2)}) copy-start(bf16[1,576,1152]{2,1,0:T(8,128)(2,1)} %param.36) | copy-start | bytes 3981316
  41.0 44.5 %all-to-all-start = ((f32[256,1,576]{2,1,0:T(1,128)}), f32[256,1,576]{2,1,0:T(1,128)S(1)}, u32[]{:S(2)}, u32[]{:S(2)}) async-start(f32[256,1,576]{2,1,0:T(1,128)} %reshape.299), calls=%async_computation | async-start | bytes 1310720 | tf_op jit(solution)/shard_map/all_to_all | solution.py:160
  61.2 178.0 %all-reduce.3.cloned.1.call-start = ((), (), s32[]{:S(2)}) async-start(), calls=%async_computation.1 | async-start | bytes 2359296 | tf_op jit(solution)/shard_map/psum | solution.py:177
  67.3 6.3 %copy-start.3 = (f32[256,1152]{1,0:T(8,128)}, f32[256,1152]{1,0:T(8,128)S(1)}, u32[]{:S(2)}) copy-start(f32[256,1152]{1,0:T(8,128)S(1)} %concatenate.6) | copy-start | bytes 3538948
  69.5 4.1 %copy-start.9 = (f32[256,2,16]{0,2,1:T(8,128)S(1)}, f32[256,2,16]{0,2,1:T(8,128)}, u32[]{:S(2)}) copy-start(f32[256,2,16]{0,2,1:T(8,128)} %param.20) | copy-start | bytes 98308
  69.5 4.2 %copy-start.17 = (f32[1,3,144]{2,0,1:T(1,128)S(1)}, f32[1,3,144]{2,0,1:T(1,128)}, u32[]{:S(2)}) copy-start(f32[1,3,144]{2,0,1:T(1,128)} %param.31) | copy-start | bytes 5188
  69.5 4.4 %copy-start.10 = (bf16[16,1152]{1,0:T(8,128)(2,1)S(1)}, bf16[16,1152]{1,0:T(8,128)(2,1)}, u32[]{:S(2)}) copy-start(bf16[16,1152]{1,0:T(8,128)(2,1)} %param.26) | copy-start | bytes 110596
  69.5 4.4 %copy-start.13 = (f32[1152]{0:T(1024)S(1)}, f32[1152]{0:T(1024)}, u32[]{:S(2)}) copy-start(f32[1152]{0:T(1024)} %param.27) | copy-start | bytes 13828
  77.6 1.4 copy-start.1
  105.5 4.3 %copy-start.6 = (bf16[1,1152,3,144]{1,3,2,0:T(8,128)(2,1)S(1)}, bf16[1,1152,3,144]{1,3,2,0:T(8,128)(2,1)}, u32[]{:S(2)}) copy-start(bf16[1,1152,3,144]{1,3,2,0:T(8,128)(2,1)} %param.30) | copy-start | bytes 2985988
  115.8 5.2 %copy-start.5 = (bf16[256,2,288]{2,1,0:T(2,128)(2,1)}, bf16[256,2,288]{2,1,0:T(2,128)(2,1)S(1)}, u32[]{:S(2)}) copy-start(bf16[256,2,288]{2,1,0:T(2,128)(2,1)S(1)} %slice.80) | copy-start | bytes 884740
  116.8 4.1 %collective-permute-start = (bf16[256,2,288]{2,1,0:T(2,128)(2,1)S(1)}, bf16[256,2,288]{2,1,0:T(2,128)(2,1)}, u32[]{:S(2)}, u32[]{:S(2)}) collective-permute-start(bf16[256,2,288]{2,1,0:T(2,128)(2,1)S(1)} %slice.80), channel_id=1, source_target_pairs={{0,8},{8,0},{16,24},{24,16},{32,40},{40,32},{48,56},{56,48},{64,72... | collective-permute-start | bytes 884744 | tf_op jit(solution)/shard_map/ppermute | solution.py:15
  125.2 31.5 %collective-permute-start.1 = (bf16[512,2,288]{0,2,1:T(8,128)(2,1)}, bf16[512,2,288]{0,2,1:T(8,128)(2,1)}, u32[]{:S(2)}, u32[]{:S(2)}) collective-permute-start(bf16[512,2,288]{0,2,1:T(8,128)(2,1)} %copy.83), channel_id=1, source_target_pairs={{0,16},{8,24},{16,0},{24,8},{32,48},{40,56},{48,32},{56,40},{64,80... | collective-permute-start | bytes 1769480 | tf_op jit(solution)/shard_map/ppermute | solution.py:15
  157.7 1.2 copy-start.12
  158.9 1.0 copy-start.8
  159.3 1.3 copy-start.7
  160.2 2.0 copy-start.14
  160.2 2.0 copy-start.18
  162.1 170.2 %all-reduce.5.cloned.1.call-start = ((), (), s32[]{:S(2)}) async-start(), calls=%async_computation.2 | async-start | bytes 2359296 | tf_op jit(solution)/shard_map/psum | solution.py:187
  164.3 4.2 %copy-start.11 = (f32[2,1,1152]{2,1,0:T(1,128)S(1)}, f32[2,1,1152]{2,1,0:T(1,128)}, u32[]{:S(2)}) copy-start(f32[2,1,1152]{2,1,0:T(1,128)} %get-tuple-element.28) | copy-start | bytes 27652
  242.4 1.4 copy-start.2
  249.9 1.4 copy-start.16
  251.4 4.1 %copy-start.15 = (f32[1,1152]{1,0:T(1,128)S(1)}, f32[1,1152]{1,0:T(1,128)}, u32[]{:S(2)}) copy-start(f32[1,1152]{1,0:T(1,128)} %param.37) | copy-start | bytes 13828
  251.4 4.1 %copy-start.20 = (f32[250,2]{0,1:T(2,128)S(1)}, f32[250,2]{0,1:T(2,128)}, u32[]{:S(2)}) copy-start(f32[250,2]{0,1:T(2,128)} %param.23) | copy-start | bytes 6004
  251.5 5.2 %copy-start.4 = (bf16[512,1152]{1,0:T(8,128)(2,1)S(1)}, bf16[512,1152]{1,0:T(8,128)(2,1)}, u32[]{:S(2)}) copy-start(bf16[512,1152]{1,0:T(8,128)(2,1)} %all-reduce.3.cloned.1.call-done) | copy-start | bytes 3538948
  256.7 77.9 %copy-start.19 = (bf16[1152,16]{0,1:T(8,128)(2,1)S(1)}, bf16[1152,16]{0,1:T(8,128)(2,1)}, u32[]{:S(2)}) copy-start(bf16[1152,16]{0,1:T(8,128)(2,1)} %param.38) | copy-start | bytes 110596
  256.7 77.9 %copy-start.21 = (f32[16]{0:T(128)S(1)}, f32[16]{0:T(128)}, u32[]{:S(2)}) copy-start(f32[16]{0:T(128)} %param.39) | copy-start | bytes 196
  335.1 5.5 %collective-permute-start.2 = (f32[32,2,8]{0,2,1:T(8,128)S(1)}, f32[32,2,8]{0,2,1:T(8,128)S(1)}, u32[]{:S(2)}, u32[]{:S(2)}) collective-permute-start(f32[32,2,8]{0,2,1:T(8,128)S(1)} %copy.98), channel_id=1, source_target_pairs={{0,256},{256,0},{1,257},{257,1},{2,258},{258,2},{3,259},{259,3},{4... | collective-permute-start | bytes 6152 | tf_op jit(solution)/shard_map/ppermute | solution.py:15
Sparse Core Ops, SparseCore 0:
  162.3 76.8 all-reduce.2
  251.4 80.9 all-reduce.4
